TPU v7x, 128 devices: a whole 4x4x4 slice. The times are simulated.
128 devices in a mesh: dp: 16 (over x, y_hi, core), mp: 8 (over y_lo, z).
Axes of the slice: x: 4, y: 4 (y_hi: 2, y_lo: 2; y = y_hi * 2 + y_lo), z: 4, core: 2. Of those that a mesh axis runs over, the one named last changes fastest.
Arguments:
- hidden: bfloat16 [16384, 2048], P(('dp', 'mp')), may hold values from -4 to 4
- norm_gains: float32 [3, 2048], replicated, may hold values from 0.5 to 1.5
- head_gains: float32 [3, 128], replicated, may hold values from 0.25 to 1.75
- query_weight: bfloat16 [2048, 2048], P(('dp', 'mp')), may hold values from -0.125 to 0.125
- kv_weight: bfloat16 [2048, 512], P(('dp', 'mp')), may hold values from -0.125 to 0.125
- out_weight: bfloat16 [2048, 2048], P(('dp', 'mp')), may hold values from -0.5 to 0.5
- gate_up: bfloat16 [128, 2048, 1536], P(('dp', 'mp')), may hold values from -0.125 to 0.125
- down_weight: bfloat16 [128, 768, 2048], P(('dp', 'mp')), may hold values from -0.21875 to 0.21875
- next_weight: bfloat16 [2048, 512], P(('dp', 'mp')), may hold values from -0.125 to 0.125
- expert_ids: int32 [16384, 8], P(('dp', 'mp')), may hold values from 0 to 127, all different within a row; in each aligned block of 128 rows (0 to 127, 128 to 255, ...) at most 10 rows name the same one
- route_weights: float32 [16384, 8], P(('dp', 'mp')), may hold values from 0.05 to 0.5
- token_request: int32 [16384], P('dp'), may hold values from 0 to 31, as said below
- request_leaf: int32 [32], replicated, may hold values from 0 to 15
- leaf_parent: int32 [16], replicated, may hold values from 0 to 7
- mid_parent: int32 [8], replicated, may hold values from 0 to 7
- root_length: int32 [8], replicated, may hold values from 1 to 512, as said below
- mid_length: int32 [8], replicated, may hold values from 1 to 256, as said below
- leaf_length: int32 [16], replicated, may hold values from 1 to 128, as said below
- root_slot: int32 [8], replicated, may hold values from 0 to 7, each once
- mid_slot: int32 [8], replicated, may hold values from 0 to 7, each once
- leaf_slot: int32 [16], replicated, may hold values from 0 to 15, each once
- root_cache: bfloat16 [8, 512, 512], P('mp'), may hold values from -300 to 300
- mid_cache: bfloat16 [8, 256, 512], P('mp'), may hold values from -300 to 300
- leaf_cache: bfloat16 [16, 128, 512], P('mp'), may hold values from -300 to 300
Outputs:
- layer_out: bfloat16 [16384, 2048], P(('dp', 'mp'))
- next_rows: bfloat16 [16384, 512], P(('dp', 'mp'))
Inputs may be any that keep to these rules, and one draw needn't show every extreme that they name: `expert_ids`: each row names 8 different experts; among the rows of one device no expert is named more than 10 times, a bound that some block reaches. `token_request`: Nondecreasing; tokens g * 1024 to (g + 1) * 1024 - 1 belong to requests g * 2 to (g + 1) * 2 - 1, and every request has at least one token. `root_length`: some root node has the full length. `mid_length`: some middle node has the full length. `leaf_length`: some leaf node has the full length. `root_slot`: each slot once; slot s is on index s // 1 of mp. `mid_slot`: each slot once; slot s is on index s // 1 of mp. `leaf_slot`: each slot once; slot s is on index s // 2 of mp.
All inputs are finite; a program needn't handle non-finite values.
Results may differ from a plain program's by a relative error of at most 0.024.
Values may be sent and summed in bfloat16 or wider, within the bound.
No kernel may reach another device: no remote copies, remote signals or barrier semaphores. Data moves between devices by JAX's collectives and lax.ppermute only.
A program may use at most 192 MiB of HBM per device.

v0:
```python
import jax
import jax.numpy as jnp
from jax import lax
from jax.sharding import PartitionSpec as P

REQ_GRP = 2
EPS = 1e-06
THETA = 1000000.0
MASKED = -1e30


def rms_norm(values, weight_row):
    values = values.astype(jnp.float32)
    return values * lax.rsqrt(jnp.mean(values * values, axis=-1, keepdims=True) + EPS) * weight_row


def rotate(values, positions):
    half_dim = values.shape[-1] // 2
    frequency = THETA ** (-2.0 * jnp.arange(half_dim, dtype=jnp.float32) / values.shape[-1])
    angles = positions.astype(jnp.float32)[:, None] * frequency[None, :]
    cosine = jnp.cos(angles)[:, None, :]
    sine_part = jnp.sin(angles)[:, None, :]
    front_part = values[..., :half_dim]
    back_part = values[..., half_dim:]
    return jnp.concatenate(
        [front_part * cosine - back_part * sine_part, back_part * cosine + front_part * sine_part],
        axis=-1,
    )


def look_up(lookup_table, indices):
    places = jnp.arange(lookup_table.shape[0], dtype=jnp.int32)
    return jnp.sum(jnp.where(indices[:, None] == places[None, :], lookup_table[None, :], 0), axis=1)


def tree_paths(requests, request_leaf, leaf_parent, mid_parent, lengths, slot_tables):
    leaf_node = look_up(request_leaf, requests)
    mid_node = look_up(leaf_parent, leaf_node)
    root_node = look_up(mid_parent, mid_node)
    node_sets = (root_node, mid_node, leaf_node)
    path_slots = [
        look_up(slot_table, node_ids) for slot_table, node_ids in zip(slot_tables, node_sets)
    ]
    path_lengths = [
        look_up(length_table, node_ids) for length_table, node_ids in zip(lengths, node_sets)
    ]
    return (path_slots, path_lengths)


def head_scores(queries, key_rows, allowed):
    kv_heads = queries.shape[1]
    head_dim = queries.shape[3]
    score_scale = head_dim ** (-0.5)
    outcome = []
    for head_no in range(kv_heads):
        key_part = key_rows[:, head_no * head_dim : (head_no + 1) * head_dim]
        raw_scores = (
            jnp.einsum(
                "ngd,pd->ngp", queries[:, head_no], key_part, preferred_element_type=jnp.float32
            )
            * score_scale
        )
        outcome.append(jnp.where(allowed[:, None, :], raw_scores, MASKED))
    return outcome


def head_peaks(score_list):
    return jnp.stack([jnp.max(scores, axis=2) for scores in score_list], axis=1)


def head_sums(score_list, row_shift, key_rows, allowed):
    kv_width = key_rows.shape[1] // 2
    head_dim = kv_width // len(score_list)
    numerators = []
    totals = []
    for head_no, scores in enumerate(score_list):
        weights = jnp.where(
            allowed[:, None, :], jnp.exp(scores - row_shift[:, head_no, :, None]), 0.0
        )
        value_part = key_rows[
            :, kv_width + head_no * head_dim : kv_width + (head_no + 1) * head_dim
        ]
        numerators.append(
            jnp.einsum(
                "ngp,pd->ngd",
                weights.astype(jnp.bfloat16),
                value_part,
                preferred_element_type=jnp.float32,
            )
        )
        totals.append(jnp.sum(weights, axis=2))
    return (jnp.stack(numerators, axis=1), jnp.stack(totals, axis=1))


def join_parts(pre_peak, pre_num, pre_total, self_peak, self_num, self_total):
    row_top = jnp.maximum(pre_peak, self_peak)
    pre_factor = jnp.exp(pre_peak - row_top)
    self_factor = jnp.exp(self_peak - row_top)
    combined = pre_num * pre_factor[..., None] + self_num * self_factor[..., None]
    divisor = pre_total * pre_factor + self_total * self_factor
    return combined / divisor[..., None]


def fold_rows(source, pieces):
    return tuple(
        (jnp.dot(source, piece_now, preferred_element_type=jnp.float32) for piece_now in pieces)
    )


def per_device(
    hidden,
    norm_gains,
    head_gains,
    query_weight,
    kv_weight,
    out_weight,
    gate_up,
    down_weight,
    next_weight,
    expert_ids,
    route_weights,
    token_request,
    request_leaf,
    leaf_parent,
    mid_parent,
    root_length,
    mid_length,
    leaf_length,
    root_slot,
    mid_slot,
    leaf_slot,
    root_cache,
    mid_cache,
    leaf_cache,
):
    tok_rows = hidden.shape[0]
    model_dim = hidden.shape[1]
    head_dim = head_gains.shape[1]
    kv_width = kv_weight.shape[1] // 2
    kv_heads = kv_width // head_dim
    query_width = query_weight.shape[1]
    head_count = query_width // head_dim
    head_ratio = head_count // kv_heads
    group_tok = token_request.shape[0]
    mp_size = lax.axis_size("mp")
    devices_all = lax.axis_size("dp") * mp_size
    my_first = lax.axis_index("mp") * tok_rows
    lengths = (root_length, mid_length, leaf_length)
    slot_tables = (root_slot, mid_slot, leaf_slot)
    my_request = lax.dynamic_slice_in_dim(token_request, my_first, tok_rows)
    request_first = jnp.sum(
        (token_request[None, :] < my_request[:, None]).astype(jnp.int32), axis=1
    )
    my_places = my_first + jnp.arange(tok_rows, dtype=jnp.int32)
    my_slots, my_lengths = tree_paths(
        my_request, request_leaf, leaf_parent, mid_parent, lengths, slot_tables
    )
    positions = my_lengths[0] + my_lengths[1] + my_lengths[2] + my_places - request_first
    normed = rms_norm(hidden, norm_gains[0]).astype(jnp.bfloat16)
    query_raw, kv_raw = fold_rows(
        normed,
        (
            lax.all_gather(query_weight, ("dp", "mp"), axis=0, tiled=True),
            lax.all_gather(kv_weight, ("dp", "mp"), axis=0, tiled=True),
        ),
    )
    queries = rotate(
        rms_norm(query_raw.reshape(tok_rows, head_count, head_dim), head_gains[0]), positions
    ).astype(jnp.bfloat16)
    new_keys = rotate(
        rms_norm(kv_raw[:, :kv_width].reshape(tok_rows, kv_heads, head_dim), head_gains[1]),
        positions,
    ).astype(jnp.bfloat16)
    new_rows = jnp.concatenate(
        [new_keys.reshape(tok_rows, kv_width), kv_raw[:, kv_width:].astype(jnp.bfloat16)], axis=1
    )
    group_rows = lax.all_gather(new_rows, "mp", axis=0, tiled=True)
    self_allowed = (my_request[:, None] == token_request[None, :]) & (
        jnp.arange(group_tok, dtype=jnp.int32)[None, :] <= my_places[:, None]
    )
    my_queries = queries.reshape(tok_rows, kv_heads, head_ratio, head_dim)
    self_scores = head_scores(my_queries, group_rows, self_allowed)
    self_peak = head_peaks(self_scores)
    self_num, self_total = head_sums(self_scores, self_peak, group_rows, self_allowed)
    gathered = (
        lax.all_gather(root_cache, "mp", axis=0, tiled=True),
        lax.all_gather(mid_cache, "mp", axis=0, tiled=True),
        lax.all_gather(leaf_cache, "mp", axis=0, tiled=True),
    )
    first_request = token_request[0]
    path_rows = []
    path_masks = []
    for request_no in range(REQ_GRP):
        request_id = first_request + request_no
        chosen_slots, chosen_lengths = tree_paths(
            jnp.reshape(request_id, (1,)),
            request_leaf,
            leaf_parent,
            mid_parent,
            lengths,
            slot_tables,
        )
        mine = my_request == request_id
        for level_no in range(3):
            level_part = gathered[level_no]
            path_rows.append(
                lax.dynamic_index_in_dim(level_part, chosen_slots[level_no][0], 0, keepdims=False)
            )
            within = jnp.arange(level_part.shape[1], dtype=jnp.int32)
            path_masks.append(mine[:, None] & (within[None, :] < chosen_lengths[level_no][0]))
    prefix_rows = jnp.concatenate(path_rows, axis=0)
    prefix_allowed = jnp.concatenate(path_masks, axis=1)
    pre_scores = head_scores(my_queries, prefix_rows, prefix_allowed)
    pre_peak = head_peaks(pre_scores)
    pre_num, pre_total = head_sums(pre_scores, pre_peak, prefix_rows, prefix_allowed)
    attended = (
        join_parts(pre_peak, pre_num, pre_total, self_peak, self_num, self_total)
        .reshape(tok_rows, query_width)
        .astype(jnp.bfloat16)
    )
    projected = fold_rows(
        attended, (lax.all_gather(out_weight, ("dp", "mp"), axis=0, tiled=True),)
    )[0]
    after_attention = (hidden.astype(jnp.float32) + projected).astype(jnp.bfloat16)
    moe_in = rms_norm(after_attention, norm_gains[1]).astype(jnp.bfloat16)
    top_k = expert_ids.shape[1]
    experts_all = gate_up.shape[0] * devices_all
    capacity = max(2, 5 * tok_rows * top_k // (4 * experts_all))
    flat_ids = expert_ids.reshape(-1)
    flat_count = flat_ids.shape[0]
    order_ids = jnp.arange(flat_count, dtype=jnp.int32)
    earlier = (flat_ids[:, None] == flat_ids[None, :]) & (order_ids[None, :] < order_ids[:, None])
    slot_no = jnp.sum(earlier.astype(jnp.int32), axis=1)
    target = flat_ids * capacity + slot_no
    spread_rows = jnp.broadcast_to(moe_in[:, None, :], (tok_rows, top_k, model_dim)).reshape(
        flat_count, model_dim
    )
    outbound = (
        jnp.zeros((experts_all * capacity, model_dim), jnp.bfloat16).at[target].set(spread_rows)
    )
    block_in = lax.all_to_all(
        outbound.reshape(devices_all, 1, capacity, model_dim),
        ("dp", "mp"),
        split_axis=0,
        concat_axis=1,
        tiled=True,
    )
    rows_in = block_in.reshape(-1, model_dim)
    gate_up_out = jnp.dot(rows_in, gate_up[0], preferred_element_type=jnp.float32)
    ff_width = down_weight.shape[1]
    active = (jax.nn.silu(gate_up_out[:, :ff_width]) * gate_up_out[:, ff_width:]).astype(
        jnp.bfloat16
    )
    served = (
        jnp.dot(active, down_weight[0], preferred_element_type=jnp.float32)
        .astype(jnp.bfloat16)
        .reshape(block_in.shape)
    )
    returned = lax.all_to_all(served, ("dp", "mp"), split_axis=1, concat_axis=0, tiled=True)
    expert_rows = returned.reshape(experts_all * capacity, model_dim)[target]
    mixture = jnp.sum(
        expert_rows.astype(jnp.float32).reshape(tok_rows, top_k, model_dim)
        * route_weights[:, :, None],
        axis=1,
    )
    layer_out = (after_attention.astype(jnp.float32) + mixture).astype(jnp.bfloat16)
    next_in = rms_norm(layer_out, norm_gains[2]).astype(jnp.bfloat16)
    next_raw = fold_rows(next_in, (lax.all_gather(next_weight, ("dp", "mp"), axis=0, tiled=True),))[
        0
    ]
    next_keys = rotate(
        rms_norm(next_raw[:, :kv_width].reshape(tok_rows, kv_heads, head_dim), head_gains[2]),
        positions,
    ).astype(jnp.bfloat16)
    next_rows = jnp.concatenate(
        [next_keys.reshape(tok_rows, kv_width), next_raw[:, kv_width:].astype(jnp.bfloat16)], axis=1
    )
    return (layer_out, next_rows)


def solution(mesh):
    placed = (
        P(("dp", "mp"), None),
        P(),
        P(),
        P(("dp", "mp"), None),
        P(("dp", "mp"), None),
        P(("dp", "mp"), None),
        P(("dp", "mp"), None, None),
        P(("dp", "mp"), None, None),
        P(("dp", "mp"), None),
        P(("dp", "mp"), None),
        P(("dp", "mp"), None),
        P("dp"),
        P(),
        P(),
        P(),
        P(),
        P(),
        P(),
        P(),
        P(),
        P(),
        P("mp", None, None),
        P("mp", None, None),
        P("mp", None, None),
    )
    return jax.shard_map(
        per_device,
        mesh=mesh,
        in_specs=placed,
        out_specs=(P(("dp", "mp"), None), P(("dp", "mp"), None)),
        check_vma=False,
    )
```

profile of v0, /device:TPU:9, one launch (start us, length us, event | category | flops | bytes accessed | tf_op | source)
XLA Modules:
  0.0 1670.7 jit_solution(7209893921031694401)
XLA Ops:
  22.1 290.2 %all-gather.17.cloned.1.call-done = bf16[2048,512]{1,0:T(8,128)(2,1)} async-done(((bf16[16,512]{1,0:T(8,128)(2,1)}), bf16[2048,512]{1,0:T(8,128)(2,1)}) %all-gather.17.cloned.1.call-update) | async-done | bytes 2097168 | tf_op jit(solution)/shard_map/all_gather | solution.py:164
  312.3 2.2 fusion.71
  321.2 2.7 select_reduce_fusion.13
  323.9 2.7 select_reduce_fusion.12
  326.6 2.7 fusion.79
  330.5 2.7 select_reduce_fusion.7
  337.0 2.7 select_reduce_fusion.6
  356.5 10.2 all-gather.11.cloned.1.call-done
  368.7 34.8 %all-gather.13.cloned.1.call-done = bf16[8,256,512]{2,1,0:T(8,128)(2,1)} async-done(((bf16[1,256,512]{2,1,0:T(8,128)(2,1)}), bf16[8,256,512]{2,1,0:T(8,128)(2,1)}) %all-gather.13.cloned.1.call-update) | async-done | bytes 2097168 | tf_op jit(solution)/shard_map/all_gather | solution.py:187
  405.2 40.7 %all-gather.15.cloned.1.call-done = bf16[16,128,512]{2,1,0:T(8,128)(2,1)} async-done(((bf16[2,128,512]{2,1,0:T(8,128)(2,1)}), bf16[16,128,512]{2,1,0:T(8,128)(2,1)}) %all-gather.15.cloned.1.call-update) | async-done | bytes 2097168 | tf_op jit(solution)/shard_map/all_gather | solution.py:188
  452.5 312.0 %all-gather.9.cloned.1.call-done = bf16[2048,2048]{1,0:T(8,128)(2,1)} async-done(((bf16[16,2048]{1,0:T(8,128)(2,1)}), bf16[2048,2048]{1,0:T(8,128)(2,1)}) %all-gather.9.cloned.1.call-update) | async-done | bytes 8388624 | tf_op jit(solution)/shard_map/all_gather | solution.py:163
  764.5 4.9 convolution_bitcast_fusion
  778.1 22.6 %all-gather.19.cloned.1.call-done = bf16[1024,512]{1,0:T(8,128)(2,1)} async-done(((bf16[128,512]{1,0:T(8,128)(2,1)}), bf16[1024,512]{1,0:T(8,128)(2,1)}) %all-gather.19.cloned.1.call-update) | async-done | bytes 1048592 | tf_op jit(solution)/shard_map/all_gather | solution.py:177
  800.7 2.3 fusion.13
  804.7 2.3 fusion.22
  808.3 3.7 fusion.5
  822.0 296.9 %all-gather.21.cloned.1.call-done = bf16[2048,2048]{1,0:T(8,128)(2,1)} async-done(((bf16[16,2048]{1,0:T(8,128)(2,1)}), bf16[2048,2048]{1,0:T(8,128)(2,1)}) %all-gather.21.cloned.1.call-update) | async-done | bytes 8388624 | tf_op jit(solution)/shard_map/all_gather | solution.py:222
  1119.0 4.9 multiply_reduce_fusion
  1125.9 10.4 scatter_custom_fusion
  1136.2 9.5 reshape.559
  1145.7 104.9 %all_to_all.8 = bf16[128,1,10,2048]{3,2,1,0:T(8,128)(2,1)} all-to-all(bf16[128,1,10,2048]{3,2,1,0:T(8,128)(2,1)} %bitcast.122), channel_id=1, replica_groups=mesh['dp'=16,'mp'=8] {'dp','mp'}, dimensions={0} | all-to-all | bytes 10485760 | tf_op jit(solution)/shard_map/all_to_all | solution.py:241
  1250.7 9.8 reshape.560
  1260.5 12.1 fusion.3
  1272.6 6.1 convolution_convert_fusion
  1278.7 9.5 reshape.561
  1288.2 8.8 all-to-all-start.1
  1297.8 104.0 %all-to-all-done.1 = bf16[1,128,10,2048]{3,2,0,1:T(8,128)(2,1)} async-done(((bf16[1,128,10,2048]{3,2,0,1:T(8,128)(2,1)}), bf16[1,128,10,2048]{3,2,0,1:T(8,128)(2,1)}, u32[]{:S(2)}, u32[]{:S(2)}) %all-to-all-start.1) | async-done | bytes 5242912 | tf_op jit(solution)/shard_map/all_to_all | solution.py:259
  1401.9 9.8 reshape.562
  1411.7 12.0 gather_fusion
  1423.7 6.6 fusion
  1431.3 226.8 %all-gather.23.cloned.1.call-done = bf16[2048,512]{1,0:T(8,128)(2,1)} async-done(((bf16[16,512]{1,0:T(8,128)(2,1)}), bf16[2048,512]{1,0:T(8,128)(2,1)}) %all-gather.23.cloned.1.call-update) | async-done | bytes 2097168 | tf_op jit(solution)/shard_map/all_gather | solution.py:268
  1658.1 2.3 fusion.59
  (148 shorter events, 70.0 us)
Async XLA Ops:
  7.2 1265.4 %copy-start = (bf16[1,768,2048]{2,1,0:T(8,128)(2,1)S(1)}, bf16[1,768,2048]{2,1,0:T(8,128)(2,1)}, u32[]{:S(2)}) copy-start(bf16[1,768,2048]{2,1,0:T(8,128)(2,1)} %param.31) | copy-start | bytes 9437188
  7.2 305.2 %all-gather.17.cloned.1.call-start = ((), (), s32[]{:S(2)}) async-start(), calls=%async_computation.6 | async-start | bytes 2113536 | tf_op jit(solution)/shard_map/all_gather | solution.py:164
  7.9 358.8 %all-gather.11.cloned.1.call-start = ((), (), s32[]{:S(2)}) async-start(), calls=%async_computation.3 | async-start | bytes 4718592 | tf_op jit(solution)/shard_map/all_gather | solution.py:186
  8.7 394.8 %all-gather.13.cloned.1.call-start = ((), (), s32[]{:S(2)}) async-start(), calls=%async_computation.4 | async-start | bytes 2359296 | tf_op jit(solution)/shard_map/all_gather | solution.py:187
  9.4 436.4 %all-gather.15.cloned.1.call-start = ((), (), s32[]{:S(2)}) async-start(), calls=%async_computation.5 | async-start | bytes 2359296 | tf_op jit(solution)/shard_map/all_gather | solution.py:188
  10.0 754.5 %all-gather.9.cloned.1.call-start = ((), (), s32[]{:S(2)}) async-start(), calls=%async_computation.2 | async-start | bytes 8454144 | tf_op jit(solution)/shard_map/all_gather | solution.py:163
  10.6 790.2 %all-gather.19.cloned.1.call-start = ((), (), s32[]{:S(2)}) async-start(), calls=%async_computation.7 | async-start | bytes 1179648 | tf_op jit(solution)/shard_map/all_gather | solution.py:177
  13.7 3.0 copy-start.18
  18.9 296.4 %copy-start.16 = (f32[128]{0:T(128)}, f32[128]{0:T(128)S(1)}, u32[]{:S(2)}) copy-start(f32[128]{0:T(128)S(1)} %add_rsqrt_fusion.5) | copy-start | bytes 1540
  20.6 332.6 %copy-start.8 = (f32[128,64]{1,0:T(8,128)}, f32[128,64]{1,0:T(8,128)S(1)}, u32[]{:S(2)}) copy-start(f32[128,64]{1,0:T(8,128)S(1)} %get-tuple-element.47) | copy-start | bytes 98308
  20.6 332.6 %copy-start.10 = (f32[128,64]{1,0:T(8,128)}, f32[128,64]{1,0:T(8,128)S(1)}, u32[]{:S(2)}) copy-start(f32[128,64]{1,0:T(8,128)S(1)} %get-tuple-element.48) | copy-start | bytes 98308
  315.3 449.2 %copy-start.17 = (f32[128]{0:T(128)S(1)}, f32[128]{0:T(128)}, u32[]{:S(2)}) copy-start(f32[128]{0:T(128)} %copy-done.16) | copy-start | bytes 1540
  318.5 800.5 %all-gather.21.cloned.1.call-start = ((), (), s32[]{:S(2)}) async-start(), calls=%async_computation.8 | async-start | bytes 8454144 | tf_op jit(solution)/shard_map/all_gather | solution.py:222
  452.5 320.7 %copy-start.21 = (f32[128]{0:T(128)S(1)}, f32[128]{0:T(128)}, u32[]{:S(2)}) copy-start(f32[128]{0:T(128)} %get-tuple-element.45) | copy-start | bytes 1540
  769.6 1.0 copy-start.3
  776.3 0.8 copy-start.4
  776.5 0.8 copy-start.6
  800.7 2.3 copy-start.5
  800.7 2.3 copy-start.7
  800.7 2.3 copy-start.12
  803.1 1.6 copy-start.13
  803.1 1.6 copy-start.14
  1119.0 5.9 copy-start.15
  1123.9 1.0 copy-start.1
  1288.2 9.5 copy-start.19
  1288.2 113.7 %all-to-all-start.1 = ((bf16[1,128,10,2048]{3,2,0,1:T(8,128)(2,1)}), bf16[1,128,10,2048]{3,2,0,1:T(8,128)(2,1)}, u32[]{:S(2)}, u32[]{:S(2)}) async-start(bf16[1,128,10,2048]{3,2,0,1:T(8,128)(2,1)} %bitcast.121), calls=%async_computation.1 | async-start | bytes 16777216 | tf_op jit(solution)/shard_map/all_to_all | solution.py:259
  1297.0 361.1 %all-gather.23.cloned.1.call-start = ((), (), s32[]{:S(2)}) async-start(), calls=%async_computation.9 | async-start | bytes 2113536 | tf_op jit(solution)/shard_map/all_gather | solution.py:268
  1423.7 6.6 copy-start.2
  1430.3 231.0 %copy-start.20 = (f32[128]{0:T(128)S(1)}, f32[128]{0:T(128)}, u32[]{:S(2)}) copy-start(f32[128]{0:T(128)} %get-tuple-element.44) | copy-start | bytes 1540
  1430.3 231.2 %copy-start.9 = (f32[128,64]{1,0:T(8,128)S(1)}, f32[128,64]{1,0:T(8,128)}, u32[]{:S(2)}) copy-start(f32[128,64]{1,0:T(8,128)} %copy-done.8) | copy-start | bytes 98308
  1430.3 231.2 %copy-start.11 = (f32[128,64]{1,0:T(8,128)S(1)}, f32[128,64]{1,0:T(8,128)}, u32[]{:S(2)}) copy-start(f32[128,64]{1,0:T(8,128)} %copy-done.10) | copy-start | bytes 98308
Sparse Core Ops, SparseCore 0:
  9.7 302.5 all-gather.16
  314.0 52.7 all-gather.10
  368.4 35.0 all-gather.12
  405.0 40.8 all-gather.14
  447.4 317.0 all-gather.8
  766.6 34.1 all-gather.18
  802.4 316.5 all-gather.20
  1299.5 358.5 all-gather.22
where the time goes:
time: 1680 us; the launch traced here: 1670 us
  waiting for transfers between devices  1340 us (80%)
  blocking collectives  105 us (6%)
  local copies, waits for them, and re-layouts  83 us (5%)
  other arithmetic  55.1 us (3%)
  matrix products  49 us (3%)
  between operations  26.7 us (2%)
    all_gather x1, waiting for transfers between devices, per_device(): lax.all_gather(query_weight, ('dp', 'mp'), axis=0, tiled=True)  312 us
    all_gather x1, waiting for transfers between devices, per_device(): lax.all_gather(out_weight, ('dp', 'mp'), axis=0, tiled=True)  297 us
    all_gather x1, waiting for transfers between devices, per_device(): lax.all_gather(kv_weight, ('dp', 'mp'), axis=0, tiled=True)  290 us
    all_gather x1, waiting for transfers between devices, per_device(): lax.all_gather(next_weight, ('dp', 'mp'), axis=0, tiled=True)  227 us
    all_to_all x1, blocking collectives, per_device(): lax.all_to_all(outbound.reshape(devices_all, 1, capacity, model_dim), ('d...  105 us
    all_to_all x1, waiting for transfers between devices, per_device(): lax.all_to_all(served, ('dp', 'mp'), split_axis=1, concat_axis=0, tiled=T...  104 us
    all_gather x1, waiting for transfers between devices, per_device(): lax.all_gather(leaf_cache, 'mp', axis=0, tiled=True)  40.7 us
    all_gather x1, waiting for transfers between devices, per_device(): lax.all_gather(mid_cache, 'mp', axis=0, tiled=True)  34.8 us
  transfers between devices with their start and end apart: 9, of which 9 were waited for; matrix products, arithmetic and copies ran while one was open for 7% of the time, Pallas kernels for 0%

commit v1 on v0

--- a/solution.py
+++ b/solution.py
@@ -256,7 +256,12 @@
         .astype(jnp.bfloat16)
         .reshape(block_in.shape)
     )
-    returned = lax.all_to_all(served, ("dp", "mp"), split_axis=1, concat_axis=0, tiled=True)
+    returned = jnp.concatenate(
+        lax.all_to_all(
+            jnp.stack(jnp.split(served, lax.axis_size(("dp", "mp")), axis=1)), ("dp", "mp"), 0, 0
+        ),
+        axis=0,
+    )
     expert_rows = returned.reshape(experts_all * capacity, model_dim)[target]
     mixture = jnp.sum(
         expert_rows.astype(jnp.float32).reshape(tok_rows, top_k, model_dim)

time: 1680 us -> 1870 us (1.11)
  local copies, waits for them, and re-layouts: 83 us -> 270 us
    unnamed x54 -> x173, local copies, waits for them, and re-layouts: 12.7 us -> 198 us
  transfers between devices with their start and end apart: 9 -> 9, of which waited for: 9 -> 9; matrix products, arithmetic and copies ran while one was open for 7% -> 6% of each run, Pallas kernels for 0% -> 0%
where the time goes in v1:
time: 1870 us; the launch traced here: 1860 us
  waiting for transfers between devices  1340 us (72%)
  local copies, waits for them, and re-layouts  270 us (14%)
  blocking collectives  104 us (6%)
  other arithmetic  56.3 us (3%)
  matrix products  50.2 us (3%)
  between operations  27 us (1%)
    all_gather x1, waiting for transfers between devices, per_device(): lax.all_gather(query_weight, ('dp', 'mp'), axis=0, tiled=True)  312 us
    all_gather x1, waiting for transfers between devices, per_device(): lax.all_gather(out_weight, ('dp', 'mp'), axis=0, tiled=True)  295 us
    all_gather x1, waiting for transfers between devices, per_device(): lax.all_gather(kv_weight, ('dp', 'mp'), axis=0, tiled=True)  290 us
    all_gather x1, waiting for transfers between devices, per_device(): lax.all_gather(next_weight, ('dp', 'mp'), axis=0, tiled=True)  227 us
    unnamed x173, local copies, waits for them, and re-layouts  198 us
    all_to_all x1, blocking collectives, per_device(): lax.all_to_all(outbound.reshape(devices_all, 1, capacity, model_dim), ('d...  104 us
    all_to_all x1, waiting for transfers between devices, per_device(): lax.all_to_all(jnp.stack(jnp.split(served, lax.axis_size(('dp', 'mp')), a...  104 us
    all_gather x1, waiting for transfers between devices, per_device(): lax.all_gather(leaf_cache, 'mp', axis=0, tiled=True)  40.7 us
  transfers between devices with their start and end apart: 9, of which 9 were waited for; matrix products, arithmetic and copies ran while one was open for 6% of the time, Pallas kernels for 0%

profile of v1, /device:TPU:9, one launch (start us, length us, event | category | flops | bytes accessed | tf_op | source)
XLA Modules:
  0.0 1858.0 jit_solution(10648028748578931182)
XLA Ops:
  22.1 290.2 %all-gather.17.cloned.1.call-done = bf16[2048,512]{1,0:T(8,128)(2,1)} async-done(((bf16[16,512]{1,0:T(8,128)(2,1)}), bf16[2048,512]{1,0:T(8,128)(2,1)}) %all-gather.17.cloned.1.call-update) | async-done | bytes 2097168 | tf_op jit(solution)/shard_map/all_gather | solution.py:164
  321.2 2.7 select_reduce_fusion.13
  323.9 2.7 select_reduce_fusion.12
  326.6 2.7 fusion.79
  330.5 2.7 select_reduce_fusion.7
  337.0 2.7 select_reduce_fusion.6
  356.5 10.2 all-gather.11.cloned.1.call-done
  368.7 34.8 %all-gather.13.cloned.1.call-done = bf16[8,256,512]{2,1,0:T(8,128)(2,1)} async-done(((bf16[1,256,512]{2,1,0:T(8,128)(2,1)}), bf16[8,256,512]{2,1,0:T(8,128)(2,1)}) %all-gather.13.cloned.1.call-update) | async-done | bytes 2097168 | tf_op jit(solution)/shard_map/all_gather | solution.py:187
  405.2 40.7 %all-gather.15.cloned.1.call-done = bf16[16,128,512]{2,1,0:T(8,128)(2,1)} async-done(((bf16[2,128,512]{2,1,0:T(8,128)(2,1)}), bf16[16,128,512]{2,1,0:T(8,128)(2,1)}) %all-gather.15.cloned.1.call-update) | async-done | bytes 2097168 | tf_op jit(solution)/shard_map/all_gather | solution.py:188
  452.5 312.0 %all-gather.9.cloned.1.call-done = bf16[2048,2048]{1,0:T(8,128)(2,1)} async-done(((bf16[16,2048]{1,0:T(8,128)(2,1)}), bf16[2048,2048]{1,0:T(8,128)(2,1)}) %all-gather.9.cloned.1.call-update) | async-done | bytes 8388624 | tf_op jit(solution)/shard_map/all_gather | solution.py:163
  764.5 4.9 convolution_bitcast_fusion
  778.1 22.6 %all-gather.19.cloned.1.call-done = bf16[1024,512]{1,0:T(8,128)(2,1)} async-done(((bf16[128,512]{1,0:T(8,128)(2,1)}), bf16[1024,512]{1,0:T(8,128)(2,1)}) %all-gather.19.cloned.1.call-update) | async-done | bytes 1048592 | tf_op jit(solution)/shard_map/all_gather | solution.py:177
  800.7 2.3 fusion.13
  803.0 2.8 fusion.1
  805.8 2.3 fusion.22
  809.4 3.7 fusion.5
  823.1 295.5 %all-gather.21.cloned.1.call-done = bf16[2048,2048]{1,0:T(8,128)(2,1)} async-done(((bf16[16,2048]{1,0:T(8,128)(2,1)}), bf16[2048,2048]{1,0:T(8,128)(2,1)}) %all-gather.21.cloned.1.call-update) | async-done | bytes 8388624 | tf_op jit(solution)/shard_map/all_gather | solution.py:222
  1118.6 4.9 multiply_reduce_fusion
  1125.5 10.4 scatter_custom_fusion
  1135.9 9.5 reshape.552
  1145.4 104.4 %all_to_all.14 = bf16[128,1,10,2048]{3,2,1,0:T(8,128)(2,1)} all-to-all(bf16[128,1,10,2048]{3,2,1,0:T(8,128)(2,1)} %bitcast.630), channel_id=1, replica_groups=mesh['dp'=16,'mp'=8] {'dp','mp'}, dimensions={0} | all-to-all | bytes 10485760 | tf_op jit(solution)/shard_map/all_to_all | solution.py:241
  1249.8 9.8 reshape.553
  1259.6 12.1 fusion.3
  1271.7 6.1 convolution_convert_fusion
  1277.8 9.5 reshape.554
  1474.4 8.6 all-to-all-start.1
  1483.8 104.0 %all-to-all-done.1 = bf16[128,1,1,10,2048]{4,3,2,1,0:T(8,128)(2,1)} async-done(((bf16[128,1,1,10,2048]{4,3,2,1,0:T(8,128)(2,1)}), bf16[128,1,1,10,2048]{4,3,2,1,0:T(8,128)(2,1)}, u32[]{:S(2)}, u32[]{:S(2)}) %all-to-all-start.1) | async-done | bytes 5242912 | tf_op jit(solution)/shard_map/all_to_all | solution.py:260
  1587.8 10.1 reshape_reshape.3
  1597.9 12.0 gather_fusion
  1610.0 6.5 fusion
  1618.7 226.5 %all-gather.23.cloned.1.call-done = bf16[2048,512]{1,0:T(8,128)(2,1)} async-done(((bf16[16,512]{1,0:T(8,128)(2,1)}), bf16[2048,512]{1,0:T(8,128)(2,1)}) %all-gather.23.cloned.1.call-update) | async-done | bytes 2097168 | tf_op jit(solution)/shard_map/all_gather | solution.py:273
  1845.2 2.3 fusion.59
  (268 shorter events, 258.9 us)
Async XLA Ops:
  7.2 1264.5 %copy-start = (bf16[1,768,2048]{2,1,0:T(8,128)(2,1)S(1)}, bf16[1,768,2048]{2,1,0:T(8,128)(2,1)}, u32[]{:S(2)}) copy-start(bf16[1,768,2048]{2,1,0:T(8,128)(2,1)} %param.31) | copy-start | bytes 9437188
  7.2 305.2 %all-gather.17.cloned.1.call-start = ((), (), s32[]{:S(2)}) async-start(), calls=%async_computation.6 | async-start | bytes 2113536 | tf_op jit(solution)/shard_map/all_gather | solution.py:164
  7.9 358.8 %all-gather.11.cloned.1.call-start = ((), (), s32[]{:S(2)}) async-start(), calls=%async_computation.3 | async-start | bytes 4718592 | tf_op jit(solution)/shard_map/all_gather | solution.py:186
  8.7 394.8 %all-gather.13.cloned.1.call-start = ((), (), s32[]{:S(2)}) async-start(), calls=%async_computation.4 | async-start | bytes 2359296 | tf_op jit(solution)/shard_map/all_gather | solution.py:187
  9.4 436.4 %all-gather.15.cloned.1.call-start = ((), (), s32[]{:S(2)}) async-start(), calls=%async_computation.5 | async-start | bytes 2359296 | tf_op jit(solution)/shard_map/all_gather | solution.py:188
  10.0 754.5 %all-gather.9.cloned.1.call-start = ((), (), s32[]{:S(2)}) async-start(), calls=%async_computation.2 | async-start | bytes 8454144 | tf_op jit(solution)/shard_map/all_gather | solution.py:163
  10.6 790.2 %all-gather.19.cloned.1.call-start = ((), (), s32[]{:S(2)}) async-start(), calls=%async_computation.7 | async-start | bytes 1179648 | tf_op jit(solution)/shard_map/all_gather | solution.py:177
  13.7 3.0 copy-start.14
  18.9 296.4 %copy-start.13 = (f32[128]{0:T(128)}, f32[128]{0:T(128)S(1)}, u32[]{:S(2)}) copy-start(f32[128]{0:T(128)S(1)} %add_rsqrt_fusion.5) | copy-start | bytes 1540
  20.6 332.6 %copy-start.5 = (f32[128,64]{1,0:T(8,128)}, f32[128,64]{1,0:T(8,128)S(1)}, u32[]{:S(2)}) copy-start(f32[128,64]{1,0:T(8,128)S(1)} %get-tuple-element.47) | copy-start | bytes 98308
  20.6 332.6 %copy-start.7 = (f32[128,64]{1,0:T(8,128)}, f32[128,64]{1,0:T(8,128)S(1)}, u32[]{:S(2)}) copy-start(f32[128,64]{1,0:T(8,128)S(1)} %get-tuple-element.48) | copy-start | bytes 98308
  318.5 800.2 %all-gather.21.cloned.1.call-start = ((), (), s32[]{:S(2)}) async-start(), calls=%async_computation.8 | async-start | bytes 8454144 | tf_op jit(solution)/shard_map/all_gather | solution.py:222
  452.5 320.7 %copy-start.17 = (f32[128]{0:T(128)S(1)}, f32[128]{0:T(128)}, u32[]{:S(2)}) copy-start(f32[128]{0:T(128)} %get-tuple-element.45) | copy-start | bytes 1540
  769.6 1.0 copy-start.2
  776.3 0.8 copy-start.3
  776.5 0.8 copy-start.4
  800.7 5.0 copy-start.10
  800.7 5.0 copy-start.11
  805.8 3.6 copy-start.9
  1118.6 5.9 copy-start.12
  1123.6 1.0 copy-start.1
  1474.4 9.3 copy-start.15
  1474.4 113.5 %all-to-all-start.1 = ((bf16[128,1,1,10,2048]{4,3,2,1,0:T(8,128)(2,1)}), bf16[128,1,1,10,2048]{4,3,2,1,0:T(8,128)(2,1)}, u32[]{:S(2)}, u32[]{:S(2)}) async-start(bf16[128,1,1,10,2048]{4,3,2,1,0:T(8,128)(2,1)} %constant_dynamic-update-slice_fusion.10), calls=%async_computation.1 | async-start | bytes 16777216 | tf_op jit(solution)/shard_map/all_to_all | solution.py:260
  1482.9 362.3 %all-gather.23.cloned.1.call-start = ((), (), s32[]{:S(2)}) async-start(), calls=%async_computation.9 | async-start | bytes 2113536 | tf_op jit(solution)/shard_map/all_gather | solution.py:273
  1609.9 238.5 %copy-start.16 = (f32[128]{0:T(128)S(1)}, f32[128]{0:T(128)}, u32[]{:S(2)}) copy-start(f32[128]{0:T(128)} %get-tuple-element.44) | copy-start | bytes 1540
  1610.0 238.7 %copy-start.6 = (f32[128,64]{1,0:T(8,128)S(1)}, f32[128,64]{1,0:T(8,128)}, u32[]{:S(2)}) copy-start(f32[128,64]{1,0:T(8,128)} %copy-done.5) | copy-start | bytes 98308
  1610.0 238.7 %copy-start.8 = (f32[128,64]{1,0:T(8,128)S(1)}, f32[128,64]{1,0:T(8,128)}, u32[]{:S(2)}) copy-start(f32[128,64]{1,0:T(8,128)} %copy-done.7) | copy-start | bytes 98308
Sparse Core Ops, SparseCore 0:
  9.7 302.5 all-gather.16
  314.0 52.7 all-gather.10
  368.4 35.0 all-gather.12
  405.0 40.8 all-gather.14
  447.4 317.0 all-gather.8
  766.6 34.1 all-gather.18
  802.4 316.1 all-gather.20
  1485.5 359.7 all-gather.22
